TPU v7x, 32 devices: a whole 2x2x4 slice. The times are simulated.
32 devices in a mesh: slab: 8 (over y, x, core), grp: 4 (over z).
Axes of the slice: x: 2, y: 2, z: 4, core: 2. Of those that a mesh axis runs over, the one named last changes fastest.
Arguments:
- near_field: bfloat16 [2, 4096, 2048], P(None, 'slab', 'grp'), may hold values from -6 to 6
- lens_phase: float32 [2, 4096, 2048], P(None, 'slab', 'grp'), may hold values from -3.140625 to 3.140625
Outputs:
- far_field: float32 [2, 512, 2048], P(None, ('slab', 'grp'))
All inputs are finite; a program needn't handle non-finite values.
Results may differ from a plain program's by a relative error of at most 0.0083.
Values may be sent and summed in bfloat16 or wider, within the bound.
A program may use at most 128 MiB of HBM per device.

v0:
```python
import math
import jax
import jax.numpy as jnp
from jax import lax
from jax.sharding import PartitionSpec as P

AV = 512
AL = 2048
PHASE_CODE = 40.0


def sincos(angle):
    half = 0.5 * angle
    sq = half * half
    sin = -1.0 / 39916800.0
    for term in (1.0 / 362880.0, -1.0 / 5040.0, 1.0 / 120.0, -1.0 / 6.0, 1.0):
        sin = sin * sq + term
    sin = sin * half
    cos = 1.0 / 479001600.0
    for term in (-1.0 / 3628800.0, 1.0 / 40320.0, -1.0 / 720.0, 1.0 / 24.0, -0.5, 1.0):
        cos = cos * sq + term
    return (1.0 - 2.0 * sin * sin, 2.0 * sin * cos)


def unit_angle(turns, modulus):
    assert modulus & modulus - 1 == 0
    centred = (turns + modulus // 2 & modulus - 1) - modulus // 2
    return sincos(centred.astype(jnp.float32) * (2.0 * math.pi / modulus))


def count(size):
    return lax.optimization_barrier(jnp.arange(size, dtype=jnp.int32))


def phase_table(row_index, col_index, modulus):
    cos, sin = unit_angle(row_index[:, None] * col_index[None, :], modulus)
    return (cos.astype(jnp.bfloat16), sin.astype(jnp.bfloat16))


def propagator(points):
    band = math.gcd(points, 128)
    offset = count(points)[None, :] - count(band)[:, None]
    cos, sin = unit_angle(offset * offset - points // 4, 2 * points)
    gain = 1.0 / math.sqrt(points)

    def rolled(part):
        part = lax.optimization_barrier((part * gain).astype(jnp.bfloat16))
        twice = jnp.concatenate([part, part], axis=1)
        return jnp.concatenate(
            [
                lax.slice_in_dim(twice, points - start, 2 * points - start, axis=1)
                for start in range(0, points, band)
            ]
        )

    return (rolled(cos), rolled(sin))


def matmul(left, right):
    return jnp.dot(left, right, preferred_element_type=jnp.float32)


def complex_product(both, table_cos, table_sin):
    rows = both.shape[0] // 2
    with_cos = matmul(both, table_cos)
    with_sin = matmul(both, table_sin)
    return (with_cos[:rows] - with_sin[rows:], with_sin[:rows] + with_cos[rows:])


def on_device(near_field, lens_phase):
    slab_count = lax.axis_size("slab")
    group_count = lax.axis_size("grp")
    devices = slab_count * group_count
    steps, lat_dev, width = lens_phase.shape
    points = width * group_count
    total_rows = lat_dev * slab_count
    rows = lat_dev // group_count
    angles = AV // devices
    coded = [jnp.exp2(lens_phase[k] * PHASE_CODE).astype(jnp.bfloat16) for k in range(steps)]
    field = lax.all_to_all(near_field, "grp", split_axis=1, concat_axis=2, tiled=True)
    coded = [lax.all_to_all(part, "grp", split_axis=0, concat_axis=1, tiled=True) for part in coded]
    prop_cos, prop_sin = propagator(points)
    both = field.reshape(2 * rows, points)
    for section in range(steps):
        real, imag = complex_product(both, prop_cos, prop_sin)
        real = real.astype(jnp.bfloat16).astype(jnp.float32)
        imag = imag.astype(jnp.bfloat16).astype(jnp.float32)
        phase = jnp.log2(coded[section].astype(jnp.float32)) * (1.0 / PHASE_CODE)
        lens_cos, lens_sin = sincos(phase)
        both = jnp.concatenate(
            [
                (real * lens_cos - imag * lens_sin).astype(jnp.bfloat16),
                (real * lens_sin + imag * lens_cos).astype(jnp.bfloat16),
            ]
        )
    vert_cos, vert_sin = phase_table(count(points) - points // 2, count(AV) - AV // 2, 2 * points)
    col_real, col_imag = complex_product(both, vert_cos, -vert_sin)
    cols = jnp.stack([col_real, col_imag]).astype(jnp.bfloat16)
    cols = jnp.transpose(cols.reshape(2, rows, devices, angles), (2, 0, 3, 1))
    got = lax.all_to_all(cols, ("slab", "grp"), split_axis=0, concat_axis=0, tiled=True)
    modulus = 2 * total_rows
    period = modulus // rows
    source = count(devices) - devices // 2
    fine = count(period)
    near = count(rows)
    coarse = count(AL // period)
    w_cos, w_sin = phase_table(source, fine, period)
    got_real = got[:, 0]
    got_imag = got[:, 1]
    ein = lambda s, l, r: jnp.einsum(s, l, r, preferred_element_type=jnp.float32)
    mid_real = ein("sam,sf->afm", got_real, w_cos) + ein("sam,sf->afm", got_imag, w_sin)
    mid_imag = ein("sam,sf->afm", got_imag, w_cos) - ein("sam,sf->afm", got_real, w_sin)
    t_cos, t_sin = unit_angle(fine[:, None] * near[None, :], modulus)
    turned_real = (mid_real * t_cos + mid_imag * t_sin).astype(jnp.bfloat16)
    turned_imag = (mid_imag * t_cos - mid_real * t_sin).astype(jnp.bfloat16)
    e_cos, e_sin = phase_table(near, coarse * period - AL // 2, modulus)
    out_real = ein("afm,mc->acf", turned_real, e_cos) + ein("afm,mc->acf", turned_imag, e_sin)
    out_imag = ein("afm,mc->acf", turned_imag, e_cos) - ein("afm,mc->acf", turned_real, e_sin)
    scale = 1.0 / math.sqrt(total_rows * points)
    return (jnp.stack([out_real, out_imag]) * scale).reshape(2, angles, AL)


def solution(mesh):
    return jax.shard_map(
        on_device,
        mesh=mesh,
        in_specs=(P(None, "slab", "grp"), P(None, "slab", "grp")),
        out_specs=P(None, ("slab", "grp"), None),
        check_vma=False,
    )
```

profile of v0, /device:TPU:0, one launch (start us, length us, event | category | flops | bytes accessed | tf_op | source)
XLA Modules:
  0.0 123.4 jit_solution(17463661891979874556)
XLA Ops:
  0.0 2.8 %exponential_convert_fusion.1 = (bf16[1,512,512]{2,1,0:T(8,128)(2,1)}, bf16[1,512,512]{2,1,0:T(8,128)(2,1)}) fusion(f32[2,512,512]{2,1,0:T(8,128)} %param.3), kind=kLoop, calls=%fused_computation.138 | loop fusion | flops 1048576 | bytes 3145728 | tf_op jit(solution)/shard_map/convert_element_type | solution.py:79
  2.8 6.3 %all-to-all-start.1 = ((bf16[4,128,512]{2,1,0:T(8,128)(2,1)}), bf16[4,128,512]{2,1,0:T(8,128)(2,1)S(1)}, u32[]{:S(2)}, u32[]{:S(2)}) async-start(bf16[4,128,512]{2,1,0:T(8,128)(2,1)} %bitcast.6), calls=%async_computation.1 | async-start | bytes 1048576 | tf_op jit(solution)/shard_map/all_to_all | solution.py:81
  9.2 1.4 %fusion.27 = (bf16[128,2048]{1,0:T(8,128)(2,1)S(1)}, bf16[128,2048]{1,0:T(8,128)(2,1)S(1)}) fusion(s32[128]{0:T(128)S(1)} %iota.18, s32[2048]{0:T(1024)S(1)} %iota.21), kind=kLoop, calls=%fused_computation.108 | loop fusion | flops 10223616 | bytes 1057280 | tf_op jit(solution)/shard_map/convert_element_type | solution.py:47
  11.3 0.9 constant_dynamic-update-slice_fusion
  12.2 1.3 %fusion.76 = bf16[2048,2048]{1,0:T(8,128)(2,1)} fusion(bf16[2048,2048]{1,0:T(8,128)(2,1)} %constant_dynamic-update-slice_fusion, bf16[128,2048]{1,0:T(8,128)(2,1)S(1)} %get-tuple-element.20), kind=kLoop, calls=%fused_computation.180 | loop fusion | flops 1048576 | bytes 1048576
  19.5 4.1 %all-to-all-done.1 = bf16[4,128,512]{2,1,0:T(8,128)(2,1)S(1)} async-done(((bf16[4,128,512]{2,1,0:T(8,128)(2,1)}), bf16[4,128,512]{2,1,0:T(8,128)(2,1)S(1)}, u32[]{:S(2)}, u32[]{:S(2)}) %all-to-all-start.1) | async-done | bytes 524320 | tf_op jit(solution)/shard_map/all_to_all | solution.py:81
  23.6 3.5 %all-to-all-start.2 = ((bf16[4,128,512]{2,1,0:T(8,128)(2,1)}), bf16[4,128,512]{2,1,0:T(8,128)(2,1)S(1)}, u32[]{:S(2)}, u32[]{:S(2)}) async-start(bf16[4,128,512]{2,1,0:T(8,128)(2,1)} %bitcast.8), calls=%async_computation.2 | async-start | bytes 1048576 | tf_op jit(solution)/shard_map/all_to_all | solution.py:81
  27.1 2.1 %copy.14 = bf16[2,512,512]{2,0,1:T(2,128)(2,1)} copy(bf16[2,512,512]{2,1,0:T(8,128)(2,1)S(1)} %copy-done.1) | data formatting | bytes 2097152 | tf_op args[0]
  31.8 9.4 %all-to-all-done.2 = bf16[4,128,512]{2,1,0:T(8,128)(2,1)S(1)} async-done(((bf16[4,128,512]{2,1,0:T(8,128)(2,1)}), bf16[4,128,512]{2,1,0:T(8,128)(2,1)S(1)}, u32[]{:S(2)}, u32[]{:S(2)}) %all-to-all-start.2) | async-done | bytes 524320 | tf_op jit(solution)/shard_map/all_to_all | solution.py:81
  41.1 3.7 %all-to-all-start = ((bf16[2,512,512]{2,0,1:T(2,128)(2,1)}), bf16[2,512,512]{2,0,1:T(2,128)(2,1)S(1)}, u32[]{:S(2)}, u32[]{:S(2)}) async-start(bf16[2,512,512]{2,0,1:T(2,128)(2,1)} %copy.14), calls=%async_computation | async-start | bytes 2097152 | tf_op jit(solution)/shard_map/all_to_all | solution.py:80
  48.5 1.2 multiply_bitcast_fusion
  49.8 20.1 %all-to-all-done = bf16[2,512,512]{2,0,1:T(2,128)(2,1)S(1)} async-done(((bf16[2,512,512]{2,0,1:T(2,128)(2,1)}), bf16[2,512,512]{2,0,1:T(2,128)(2,1)S(1)}, u32[]{:S(2)}, u32[]{:S(2)}) %all-to-all-start) | async-done | bytes 1048608 | tf_op jit(solution)/shard_map/all_to_all | solution.py:80
  71.0 5.9 %convolution_bitcast_fusion = f32[256,2048]{1,0:T(8,128)S(1)} fusion(bf16[256,2048]{1,0:T(8,128)(2,1)S(1)} %bitcast.77, bf16[2048,2048]{1,0:T(8,128)(2,1)} %copy-done.2), kind=kOutput, calls=%fused_computation.69 | convolution fusion | flops 2147483648 | bytes 11534336 | tf_op jit(solution)/shard_map/dot_general | solution.py:60
  76.9 5.9 %convolution_bitcast_fusion.1 = f32[256,2048]{1,0:T(8,128)S(1)} fusion(bf16[256,2048]{1,0:T(8,128)(2,1)S(1)} %bitcast.78, bf16[2048,2048]{1,0:T(8,128)(2,1)} %fusion.102), kind=kOutput, calls=%fused_computation.70 | convolution fusion | flops 2147483648 | bytes 11534336 | tf_op jit(solution)/shard_map/dot_general | solution.py:60
  82.8 1.2 fusion.16
  84.0 1.1 fusion.18
  85.2 2.4 %fusion.43 = f32[256,2048]{1,0:T(8,128)S(1)} fusion(bf16[2048,2048]{1,0:T(8,128)(2,1)S(1)} %bitcast.82, bf16[128,2048]{1,0:T(8,128)(2,1)S(1)} %fusion.18, bf16[128,2048]{1,0:T(8,128)(2,1)S(1)} %get-tuple-element.8), kind=kOutput, calls=%fused_computation.147 | convolution fusion | flops 2149580800 | bytes 11534336 | tf_op jit(solution)/shard_map/dot_general | solution.py:60
  87.6 5.7 %fusion.44 = f32[256,2048]{1,0:T(8,128)S(1)} fusion(bf16[2048,2048]{1,0:T(8,128)(2,1)} %fusion.102, bf16[128,2048]{1,0:T(8,128)(2,1)S(1)} %fusion.18, bf16[128,2048]{1,0:T(8,128)(2,1)S(1)} %get-tuple-element.8), kind=kOutput, calls=%fused_computation.148 | convolution fusion | flops 2149580800 | bytes 11534336 | tf_op jit(solution)/shard_map/dot_general | solution.py:60
  93.3 1.4 %fusion.20 = (bf16[128,2048]{1,0:T(8,128)(2,1)S(1)}, bf16[128,2048]{1,0:T(8,128)(2,1)S(1)}, bf16[128,2048]{1,0:T(8,128)(2,1)S(1)}) fusion(f32[128,2048]{1,0:T(8,128)S(1)} %bitcast.71, f32[256,2048]{1,0:T(8,128)S(1)} %fusion.44, f32[256,2048]{1,0:T(8,128)S(1)} %fusion.43), kind=kLoop, calls=%fused_computation.101 | loop fusion | flops 9961472 | bytes 6815744 | tf_op jit(solution)/shard_map/convert_element_type | solution.py:92
  94.7 1.1 fusion.22
  95.9 3.4 %fusion.6 = f32[256,512]{1,0:T(8,128)S(1)} fusion(s32[512]{0:T(512)S(1)} %broadcast_add_fusion.1, s32[2048]{0:T(1024)S(1)} %broadcast_add_fusion, bf16[128,2048]{1,0:T(8,128)(2,1)S(1)} %fusion.22, bf16[128,2048]{1,0:T(8,128)(2,1)S(1)} %get-tuple-element.5), kind=kOutput, calls=%fused_computation.71 | convolution fusion | flops 562036736 | bytes 1583104 | tf_op jit(solution)/shard_map/dot_general | solution.py:60
  99.3 5.0 %fusion.8 = f32[256,512]{1,0:T(8,128)S(1)} fusion(s32[512]{0:T(512)S(1)} %broadcast_add_fusion.1, s32[2048]{0:T(1024)S(1)} %broadcast_add_fusion, bf16[128,2048]{1,0:T(8,128)(2,1)S(1)} %fusion.22, bf16[128,2048]{1,0:T(8,128)(2,1)S(1)} %get-tuple-element.5), kind=kOutput, calls=%fused_computation.72 | convolution fusion | flops 576716800 | bytes 1583104 | tf_op jit(solution)/shard_map/dot_general | solution.py:60
  105.5 3.7 %all-to-all-start.3 = ((bf16[32,2,16,128]{3,2,1,0:T(8,128)(2,1)}), bf16[32,2,16,128]{3,2,1,0:T(8,128)(2,1)S(1)}, u32[]{:S(2)}, u32[]{:S(2)}) async-start(bf16[32,2,16,128]{3,2,1,0:T(8,128)(2,1)} %copy.20), calls=%async_computation.3 | async-start | bytes 524288 | tf_op jit(solution)/shard_map/all_to_all | solution.py:100
  109.3 10.1 %all-to-all-done.3 = bf16[32,2,16,128]{3,2,1,0:T(8,128)(2,1)S(1)} async-done(((bf16[32,2,16,128]{3,2,1,0:T(8,128)(2,1)}), bf16[32,2,16,128]{3,2,1,0:T(8,128)(2,1)S(1)}, u32[]{:S(2)}, u32[]{:S(2)}) %all-to-all-start.3) | async-done | bytes 262176 | tf_op jit(solution)/shard_map/all_to_all | solution.py:100
  (72 shorter events, 19.1 us)
Async XLA Ops:
  2.8 20.8 %all-to-all-start.1 = ((bf16[4,128,512]{2,1,0:T(8,128)(2,1)}), bf16[4,128,512]{2,1,0:T(8,128)(2,1)S(1)}, u32[]{:S(2)}, u32[]{:S(2)}) async-start(bf16[4,128,512]{2,1,0:T(8,128)(2,1)} %bitcast.6), calls=%async_computation.1 | async-start | bytes 1048576 | tf_op jit(solution)/shard_map/all_to_all | solution.py:81
  11.3 7.3 %copy-start.2 = (bf16[2048,2048]{1,0:T(8,128)(2,1)}, bf16[2048,2048]{1,0:T(8,128)(2,1)S(1)}, u32[]{:S(2)}) copy-start(bf16[2048,2048]{1,0:T(8,128)(2,1)S(1)} %fusion.101) | copy-start | bytes 25165828
  13.6 13.6 %copy-start.1 = (bf16[2,512,512]{2,1,0:T(8,128)(2,1)S(1)}, bf16[2,512,512]{2,1,0:T(8,128)(2,1)}, u32[]{:S(2)}) copy-start(bf16[2,512,512]{2,1,0:T(8,128)(2,1)} %param.2) | copy-start | bytes 3145732
  23.6 17.5 %all-to-all-start.2 = ((bf16[4,128,512]{2,1,0:T(8,128)(2,1)}), bf16[4,128,512]{2,1,0:T(8,128)(2,1)S(1)}, u32[]{:S(2)}, u32[]{:S(2)}) async-start(bf16[4,128,512]{2,1,0:T(8,128)(2,1)} %bitcast.8), calls=%async_computation.2 | async-start | bytes 1048576 | tf_op jit(solution)/shard_map/all_to_all | solution.py:81
  41.1 7.1 %copy-start = (bf16[4,128,512]{2,1,0:T(8,128)(2,1)}, bf16[4,128,512]{2,1,0:T(8,128)(2,1)S(1)}, u32[]{:S(2)}) copy-start(bf16[4,128,512]{2,1,0:T(8,128)(2,1)S(1)} %all-to-all-done.2) | copy-start | bytes 1572868
  41.1 28.8 %all-to-all-start = ((bf16[2,512,512]{2,0,1:T(2,128)(2,1)}), bf16[2,512,512]{2,0,1:T(2,128)(2,1)S(1)}, u32[]{:S(2)}, u32[]{:S(2)}) async-start(bf16[2,512,512]{2,0,1:T(2,128)(2,1)} %copy.14), calls=%async_computation | async-start | bytes 2097152 | tf_op jit(solution)/shard_map/all_to_all | solution.py:80
  71.0 14.2 %slice-start = ((s8[8388608]{0:T(1024)(128)(4,1)}), s8[4194304]{0:T(1024)(128)(4,1)S(1)}, s32[]{:S(2)}) async-start(s8[8388608]{0:T(1024)(128)(4,1)} %bitcast.81), calls=%async_computation.4 | async-start | bytes 8388608
  76.9 8.3 %slice-start.1 = ((s8[8388608]{0:T(1024)(128)(4,1)}), s8[4194304]{0:T(1024)(128)(4,1)S(1)}, s32[]{:S(2)}) async-start(s8[8388608]{0:T(1024)(128)(4,1)} %bitcast.81), calls=%async_computation.5 | async-start | bytes 8388608
  105.5 13.9 %all-to-all-start.3 = ((bf16[32,2,16,128]{3,2,1,0:T(8,128)(2,1)}), bf16[32,2,16,128]{3,2,1,0:T(8,128)(2,1)S(1)}, u32[]{:S(2)}, u32[]{:S(2)}) async-start(bf16[32,2,16,128]{3,2,1,0:T(8,128)(2,1)} %copy.20), calls=%async_computation.3 | async-start | bytes 524288 | tf_op jit(solution)/shard_map/all_to_all | solution.py:100
where the time goes:
time: 124 us; the launch traced here: 123 us
  waiting for transfers between devices  43.7 us (35%)
  matrix products  31.3 us (25%)
  other arithmetic  25.2 us (20%)
  starting transfers between devices  17.2 us (14%)
  local copies, waits for them, and re-layouts  5.58 us (4%)
    dot_general x6, matrix products, matmul(): return jnp.dot(left, right, preferred_element_type=jnp.float32)  28.3 us
    all_to_all x1, waiting for transfers between devices, on_device(): lax.all_to_all(near_field, 'grp', split_axis=1, concat_axis=2, tiled=True)  20.1 us
    unnamed x31, other arithmetic  14.3 us
    all_to_all x2, waiting for transfers between devices, on_device(): lax.all_to_all(part, 'grp', split_axis=0, concat_axis=1, tiled=True)  13.5 us
    all_to_all x1, waiting for transfers between devices, on_device(): lax.all_to_all(cols, ('slab', 'grp'), split_axis=0, concat_axis=0, tiled=...  10.1 us
    all_to_all x2, starting transfers between devices, on_device(): lax.all_to_all(part, 'grp', split_axis=0, concat_axis=1, tiled=True)  9.82 us
    all_to_all x1, starting transfers between devices, on_device(): lax.all_to_all(cols, ('slab', 'grp'), split_axis=0, concat_axis=0, tiled=...  3.71 us
    all_to_all x1, starting transfers between devices, on_device(): lax.all_to_all(near_field, 'grp', split_axis=1, concat_axis=2, tiled=True)  3.7 us
  transfers between devices with their start and end apart: 4, of which 4 were waited for; matrix products, arithmetic and copies ran while one was open for 16% of the time, Pallas kernels for 0%

commit v1 on v0

--- a/solution.py
+++ b/solution.py
@@ -7,6 +7,29 @@
 AV = 512
 AL = 2048
 PHASE_CODE = 40.0
+
+
+def in_blocks(array, dim, size):
+    dims = array.shape
+    blocks = array.reshape(*dims[:dim], size, dims[dim] // size, *dims[dim + 1 :])
+    return jnp.moveaxis(blocks, dim, 0)
+
+
+def laid_out(tiles, dim):
+    shape = list(tiles.shape[1:])
+    shape[dim] *= tiles.shape[0]
+    return jnp.moveaxis(tiles, 0, dim).reshape(shape)
+
+
+def pairwise_exchange(shard, axis, split_dim, concat_dim):
+    peers, index = (lax.axis_size(axis), lax.axis_index(axis))
+    tiles = in_blocks(shard, split_dim, peers)
+    outs = [tiles[index]]
+    for lap in range(1, peers):
+        sent = tiles[index ^ lap]
+        outs.append(lax.ppermute(sent, axis, [(i, i ^ lap) for i in range(peers)]))
+    tiles = jnp.stack(outs)[index ^ jnp.arange(peers)]
+    return laid_out(tiles, concat_dim)
 
 
 def sincos(angle):
@@ -77,7 +100,7 @@
     rows = lat_dev // group_count
     angles = AV // devices
     coded = [jnp.exp2(lens_phase[k] * PHASE_CODE).astype(jnp.bfloat16) for k in range(steps)]
-    field = lax.all_to_all(near_field, "grp", split_axis=1, concat_axis=2, tiled=True)
+    field = pairwise_exchange(near_field, "grp", 1, 2)
     coded = [lax.all_to_all(part, "grp", split_axis=0, concat_axis=1, tiled=True) for part in coded]
     prop_cos, prop_sin = propagator(points)
     both = field.reshape(2 * rows, points)

time: 124 us -> 99.5 us (0.80)
  waiting for transfers between devices: 43.7 us -> 19.1 us
  other arithmetic: 25.2 us -> 11.5 us
  starting transfers between devices: 17.2 us -> 27 us
  local copies, waits for them, and re-layouts: 5.58 us -> 10 us
    all_to_all x1 -> x0, waiting for transfers between devices: 20.1 us -> none  [on_device(): lax.all_to_all(near_field, 'grp', split_axis=1, concat_axis=2, tiled=True)]
    unnamed x31 -> x32, other arithmetic: 14.3 us -> 1.38 us
    all_to_all x2, waiting for transfers between devices: 13.5 us -> 1.11 us  [on_device(): lax.all_to_all(part, 'grp', split_axis=0, concat_axis=1, tiled=True)]
    ppermute x0 -> x3, waiting for transfers between devices: none -> 7.89 us  [pairwise_exchange(): outs.append(lax.ppermute(sent, axis, [(i, i ^ lap) for i in range(peers)]))]
    ppermute x0 -> x3, starting transfers between devices: none -> 5.71 us  [pairwise_exchange(): outs.append(lax.ppermute(sent, axis, [(i, i ^ lap) for i in range(peers)]))]
    all_to_all x2, starting transfers between devices: 9.82 us -> 15.2 us  [on_device(): lax.all_to_all(part, 'grp', split_axis=0, concat_axis=1, tiled=True)]
    all_to_all x1 -> x0, starting transfers between devices: 3.7 us -> none  [on_device(): lax.all_to_all(near_field, 'grp', split_axis=1, concat_axis=2, tiled=True)]
    unnamed x14 -> x19, local copies, waits for them, and re-layouts: 3.35 us -> 5.86 us
  transfers between devices with their start and end apart: 4 -> 6, of which waited for: 4 -> 3; matrix products, arithmetic and copies ran while one was open for 16% -> 30% of each run, Pallas kernels for 0% -> 0%
where the time goes in v1:
time: 99.5 us; the launch traced here: 99.1 us
  matrix products  30.9 us (31%)
  starting transfers between devices  27 us (27%)
  waiting for transfers between devices  19.1 us (19%)
  other arithmetic  11.5 us (12%)
  local copies, waits for them, and re-layouts  10 us (10%)
    dot_general x6, matrix products, matmul(): return jnp.dot(left, right, preferred_element_type=jnp.float32)  28 us
    all_to_all x2, starting transfers between devices, on_device(): lax.all_to_all(part, 'grp', split_axis=0, concat_axis=1, tiled=True)  15.2 us
    all_to_all x1, waiting for transfers between devices, on_device(): lax.all_to_all(cols, ('slab', 'grp'), split_axis=0, concat_axis=0, tiled=...  10.1 us
    ppermute x3, waiting for transfers between devices, pairwise_exchange(): outs.append(lax.ppermute(sent, axis, [(i, i ^ lap) for i in range(peers)]))  7.89 us
    all_to_all x1, starting transfers between devices, on_device(): lax.all_to_all(cols, ('slab', 'grp'), split_axis=0, concat_axis=0, tiled=...  6.07 us
    unnamed x19, local copies, waits for them, and re-layouts  5.86 us
    ppermute x3, starting transfers between devices, pairwise_exchange(): outs.append(lax.ppermute(sent, axis, [(i, i ^ lap) for i in range(peers)]))  5.71 us
    dot_general x8, matrix products, on_device(): jnp.einsum(s, l, r, preferred_element_type=jnp.float32)  2.95 us
  transfers between devices with their start and end apart: 6, of which 3 were waited for; matrix products, arithmetic and copies ran while one was open for 30% of the time, Pallas kernels for 0%

profile of v1, /device:TPU:0, one launch (start us, length us, event | category | flops | bytes accessed | tf_op | source)
XLA Modules:
  0.0 99.1 jit_solution(3800332659667220720)
XLA Ops:
  0.0 1.3 %dynamic-slice_bitcast_fusion.3 = (bf16[1,2,128,512]{3,2,1,0:T(8,128)(2,1)S(1)}, bf16[2,128,512]{2,1,0:T(8,128)(2,1)S(1)}, bf16[2,128,512]{2,1,0:T(8,128)(2,1)S(1)}, bf16[2,128,512]{2,1,0:T(8,128)(2,1)S(1)}) fusion(bf16[2,4,128,512]{3,2,1,0:T(8,128)(2,1)} %bitcast.95, s32[]{:T(128)S(6)} %select_n.22, s32[]{:T(128)S(6)} %select_n.24, s32[]{:T(128)S(6)} %select_n.23, ...), kind=kLoop, calls=%fused_computation.222 | loop fusion | bytes 2097168 | tf_op jit(solution)/shard_map/dynamic_slice | solution.py:27
  1.3 3.1 %collective-permute-start = (bf16[2,128,512]{2,1,0:T(8,128)(2,1)S(1)}, bf16[2,128,512]{2,1,0:T(8,128)(2,1)S(1)}, u32[]{:S(2)}, u32[]{:S(2)}) collective-permute-start(bf16[2,128,512]{2,1,0:T(8,128)(2,1)S(1)} %get-tuple-element.19), channel_id=1, source_target_pairs={{0,1},{1,0},{2,3},{3,2},{4,5},{5,4},{6,7},{7,6},{8,9},{9,8},{10,11... | collective-permute-start | bytes 786440 | tf_op jit(solution)/shard_map/ppermute | solution.py:30
  4.4 2.6 %collective-permute-start.1 = (bf16[2,128,512]{2,1,0:T(8,128)(2,1)S(1)}, bf16[2,128,512]{2,1,0:T(8,128)(2,1)S(1)}, u32[]{:S(2)}, u32[]{:S(2)}) collective-permute-start(bf16[2,128,512]{2,1,0:T(8,128)(2,1)S(1)} %get-tuple-element.18), channel_id=1, source_target_pairs={{0,2},{1,3},{2,0},{3,1},{4,6},{5,7},{6,4},{7,5},{8,10},{9,11},{10,... | collective-permute-start | bytes 786440 | tf_op jit(solution)/shard_map/ppermute | solution.py:30
  7.0 2.8 %exponential_convert_fusion.1 = (bf16[1,512,512]{2,1,0:T(8,128)(2,1)}, bf16[1,512,512]{2,1,0:T(8,128)(2,1)}) fusion(f32[2,512,512]{2,1,0:T(8,128)} %param.3), kind=kLoop, calls=%fused_computation.138 | loop fusion | flops 1048576 | bytes 3145728 | tf_op jit(solution)/shard_map/convert_element_type | solution.py:102
  9.8 5.1 %all-to-all-start = ((bf16[4,128,512]{2,1,0:T(8,128)(2,1)}), bf16[4,128,512]{2,1,0:T(8,128)(2,1)S(1)}, u32[]{:S(2)}, u32[]{:S(2)}) async-start(bf16[4,128,512]{2,1,0:T(8,128)(2,1)} %bitcast.12), calls=%async_computation | async-start | bytes 1048576 | tf_op jit(solution)/shard_map/all_to_all | solution.py:104
  15.0 1.4 %fusion.27 = (bf16[128,2048]{1,0:T(8,128)(2,1)S(1)}, bf16[128,2048]{1,0:T(8,128)(2,1)S(1)}) fusion(s32[128]{0:T(128)S(1)} %iota.22, s32[2048]{0:T(1024)S(1)} %iota.26), kind=kLoop, calls=%fused_computation.107 | loop fusion | flops 10223616 | bytes 1057280 | tf_op jit(solution)/shard_map/convert_element_type | solution.py:70
  17.5 2.8 %copy-done.2 = bf16[2048,2048]{1,0:T(8,128)(2,1)} copy-done((bf16[2048,2048]{1,0:T(8,128)(2,1)}, bf16[2048,2048]{1,0:T(8,128)(2,1)S(1)}, u32[]{:S(2)}) %copy-start.2) | copy-done | bytes 8388632
  20.7 7.9 %collective-permute-done.1 = bf16[2,128,512]{2,1,0:T(8,128)(2,1)S(1)} collective-permute-done((bf16[2,128,512]{2,1,0:T(8,128)(2,1)S(1)}, bf16[2,128,512]{2,1,0:T(8,128)(2,1)S(1)}, u32[]{:S(2)}, u32[]{:S(2)}) %collective-permute-start.1) | collective-permute-done | bytes 262176 | tf_op jit(solution)/shard_map/ppermute | solution.py:30
  30.5 5.9 %fusion.294 = f32[256,2048]{1,0:T(8,128)S(1)} fusion(bf16[256,2048]{1,0:T(8,128)(2,1)S(1)} %bitcast.96, bf16[2048,2048]{1,0:T(8,128)(2,1)} %copy-done.2), kind=kOutput, calls=%fused_computation.427 | convolution fusion | flops 2147483648 | bytes 11534336 | tf_op jit(solution)/shard_map/dot_general | solution.py:83
  36.4 3.8 %fusion.293 = f32[256,2048]{1,0:T(8,128)} fusion(bf16[256,2048]{1,0:T(8,128)(2,1)S(1)} %bitcast.97, bf16[2048,2048]{1,0:T(8,128)(2,1)S(1)} %bitcast.104), kind=kOutput, calls=%fused_computation.426 | convolution fusion | flops 2147483648 | bytes 11534336 | tf_op jit(solution)/shard_map/dot_general | solution.py:83
  40.2 1.1 %all-to-all-done = bf16[4,128,512]{2,1,0:T(8,128)(2,1)S(1)} async-done(((bf16[4,128,512]{2,1,0:T(8,128)(2,1)}), bf16[4,128,512]{2,1,0:T(8,128)(2,1)S(1)}, u32[]{:S(2)}, u32[]{:S(2)}) %all-to-all-start) | async-done | bytes 524320 | tf_op jit(solution)/shard_map/all_to_all | solution.py:104
  41.3 10.2 %all-to-all-start.1 = ((bf16[4,128,512]{2,1,0:T(8,128)(2,1)}), bf16[4,128,512]{2,1,0:T(8,128)(2,1)S(1)}, u32[]{:S(2)}, u32[]{:S(2)}) async-start(bf16[4,128,512]{2,1,0:T(8,128)(2,1)} %bitcast.94), calls=%async_computation.1 | async-start | bytes 1048576 | tf_op jit(solution)/shard_map/all_to_all | solution.py:104
  51.7 1.3 %copy-done = f32[256,2048]{1,0:T(8,128)S(1)} copy-done((f32[256,2048]{1,0:T(8,128)S(1)}, f32[256,2048]{1,0:T(8,128)}, u32[]{:S(2)}) %copy-start) | copy-done | bytes 2097176
  53.0 1.2 %fusion.16 = (bf16[128,2048]{1,0:T(8,128)(2,1)S(1)}, bf16[128,2048]{1,0:T(8,128)(2,1)S(1)}, bf16[128,2048]{1,0:T(8,128)(2,1)S(1)}) fusion(f32[128,2048]{1,0:T(8,128)S(1)} %bitcast.88, f32[256,2048]{1,0:T(8,128)S(1)} %copy-done, f32[256,2048]{1,0:T(8,128)S(1)} %fusion.294), kind=kLoop, calls=%fused_computation.96 | loop fusion | flops 9961472 | bytes 6815744 | tf_op jit(solution)/shard_map/convert_element_type | solution.py:115
  54.2 1.1 %fusion.18 = bf16[128,2048]{1,0:T(8,128)(2,1)S(1)} fusion(bf16[128,2048]{1,0:T(8,128)(2,1)S(1)} %get-tuple-element.10, bf16[128,2048]{1,0:T(8,128)(2,1)S(1)} %get-tuple-element.9, f32[128,2048]{1,0:T(8,128)S(1)} %bitcast.89), kind=kLoop, calls=%fused_computation.98 | loop fusion | flops 8912896 | bytes 2621440 | tf_op jit(solution)/shard_map/convert_element_type | solution.py:116
  55.4 5.9 %fusion.43 = f32[256,2048]{1,0:T(8,128)S(1)} fusion(bf16[2048,2048]{1,0:T(8,128)(2,1)} %copy-done.2, bf16[128,2048]{1,0:T(8,128)(2,1)S(1)} %fusion.18, bf16[128,2048]{1,0:T(8,128)(2,1)S(1)} %get-tuple-element.8), kind=kOutput, calls=%fused_computation.147 | convolution fusion | flops 2149580800 | bytes 11534336 | tf_op jit(solution)/shard_map/dot_general | solution.py:83
  61.3 3.8 %fusion.44 = f32[256,2048]{1,0:T(8,128)} fusion(bf16[2048,2048]{1,0:T(8,128)(2,1)S(1)} %bitcast.106, bf16[128,2048]{1,0:T(8,128)(2,1)S(1)} %fusion.18, bf16[128,2048]{1,0:T(8,128)(2,1)S(1)} %get-tuple-element.8), kind=kOutput, calls=%fused_computation.148 | convolution fusion | flops 2149580800 | bytes 11534336 | tf_op jit(solution)/shard_map/dot_general | solution.py:83
  65.3 1.3 %copy-done.1 = f32[256,2048]{1,0:T(8,128)S(1)} copy-done((f32[256,2048]{1,0:T(8,128)S(1)}, f32[256,2048]{1,0:T(8,128)}, u32[]{:S(2)}) %copy-start.1) | copy-done | bytes 2097176
  66.7 1.2 %fusion.20 = (bf16[128,2048]{1,0:T(8,128)(2,1)S(1)}, bf16[128,2048]{1,0:T(8,128)(2,1)S(1)}, bf16[128,2048]{1,0:T(8,128)(2,1)S(1)}) fusion(f32[128,2048]{1,0:T(8,128)S(1)} %bitcast.90, f32[256,2048]{1,0:T(8,128)S(1)} %copy-done.1, f32[256,2048]{1,0:T(8,128)S(1)} %fusion.43), kind=kLoop, calls=%fused_computation.100 | loop fusion | flops 9961472 | bytes 6815744 | tf_op jit(solution)/shard_map/convert_element_type | solution.py:115
  67.9 1.1 %fusion.22 = bf16[128,2048]{1,0:T(8,128)(2,1)S(1)} fusion(bf16[128,2048]{1,0:T(8,128)(2,1)S(1)} %get-tuple-element.7, bf16[128,2048]{1,0:T(8,128)(2,1)S(1)} %get-tuple-element.6, f32[128,2048]{1,0:T(8,128)S(1)} %bitcast.91), kind=kLoop, calls=%fused_computation.102 | loop fusion | flops 8912896 | bytes 2621440 | tf_op jit(solution)/shard_map/convert_element_type | solution.py:116
  69.0 3.6 %fusion.6 = f32[256,512]{1,0:T(8,128)S(1)} fusion(s32[512]{0:T(512)S(1)} %broadcast_add_fusion.1, s32[2048]{0:T(1024)S(1)} %broadcast_add_fusion, bf16[128,2048]{1,0:T(8,128)(2,1)S(1)} %fusion.22, bf16[128,2048]{1,0:T(8,128)(2,1)S(1)} %get-tuple-element.5), kind=kOutput, calls=%fused_computation.70 | convolution fusion | flops 562036736 | bytes 1583104 | tf_op jit(solution)/shard_map/dot_general | solution.py:83
  72.6 5.0 %fusion.8 = f32[256,512]{1,0:T(8,128)S(1)} fusion(s32[512]{0:T(512)S(1)} %broadcast_add_fusion.1, s32[2048]{0:T(1024)S(1)} %broadcast_add_fusion, bf16[128,2048]{1,0:T(8,128)(2,1)S(1)} %fusion.22, bf16[128,2048]{1,0:T(8,128)(2,1)S(1)} %get-tuple-element.5), kind=kOutput, calls=%fused_computation.71 | convolution fusion | flops 576716800 | bytes 1583104 | tf_op jit(solution)/shard_map/dot_general | solution.py:83
  78.8 6.1 %all-to-all-start.2 = ((bf16[32,2,16,128]{3,2,1,0:T(8,128)(2,1)}), bf16[32,2,16,128]{3,2,1,0:T(8,128)(2,1)S(1)}, u32[]{:S(2)}, u32[]{:S(2)}) async-start(bf16[32,2,16,128]{3,2,1,0:T(8,128)(2,1)} %copy.33), calls=%async_computation.2 | async-start | bytes 524288 | tf_op jit(solution)/shard_map/all_to_all | solution.py:123
  85.0 10.1 %all-to-all-done.2 = bf16[32,2,16,128]{3,2,1,0:T(8,128)(2,1)S(1)} async-done(((bf16[32,2,16,128]{3,2,1,0:T(8,128)(2,1)}), bf16[32,2,16,128]{3,2,1,0:T(8,128)(2,1)S(1)}, u32[]{:S(2)}, u32[]{:S(2)}) %all-to-all-start.2) | async-done | bytes 262176 | tf_op jit(solution)/shard_map/all_to_all | solution.py:123
  (87 shorter events, 8.8 us)
Async XLA Ops:
  1.3 19.4 %collective-permute-start = (bf16[2,128,512]{2,1,0:T(8,128)(2,1)S(1)}, bf16[2,128,512]{2,1,0:T(8,128)(2,1)S(1)}, u32[]{:S(2)}, u32[]{:S(2)}) collective-permute-start(bf16[2,128,512]{2,1,0:T(8,128)(2,1)S(1)} %get-tuple-element.19), channel_id=1, source_target_pairs={{0,1},{1,0},{2,3},{3,2},{4,5},{5,4},{6,7},{7,6},{8,9},{9,8},{10,11... | collective-permute-start | bytes 786440 | tf_op jit(solution)/shard_map/ppermute | solution.py:30
  4.4 24.2 %collective-permute-start.1 = (bf16[2,128,512]{2,1,0:T(8,128)(2,1)S(1)}, bf16[2,128,512]{2,1,0:T(8,128)(2,1)S(1)}, u32[]{:S(2)}, u32[]{:S(2)}) collective-permute-start(bf16[2,128,512]{2,1,0:T(8,128)(2,1)S(1)} %get-tuple-element.18), channel_id=1, source_target_pairs={{0,2},{1,3},{2,0},{3,1},{4,6},{5,7},{6,4},{7,5},{8,10},{9,11},{10,... | collective-permute-start | bytes 786440 | tf_op jit(solution)/shard_map/ppermute | solution.py:30
  7.0 21.6 %collective-permute-start.2 = (bf16[2,128,512]{2,1,0:T(8,128)(2,1)S(1)}, bf16[2,128,512]{2,1,0:T(8,128)(2,1)S(1)}, u32[]{:S(2)}, u32[]{:S(2)}) collective-permute-start(bf16[2,128,512]{2,1,0:T(8,128)(2,1)S(1)} %get-tuple-element.20), channel_id=1, source_target_pairs={{0,3},{1,2},{2,1},{3,0},{4,7},{5,6},{6,5},{7,4},{8,11},{9,10},{10,... | collective-permute-start | bytes 786440 | tf_op jit(solution)/shard_map/ppermute | solution.py:30
  9.8 31.4 %all-to-all-start = ((bf16[4,128,512]{2,1,0:T(8,128)(2,1)}), bf16[4,128,512]{2,1,0:T(8,128)(2,1)S(1)}, u32[]{:S(2)}, u32[]{:S(2)}) async-start(bf16[4,128,512]{2,1,0:T(8,128)(2,1)} %bitcast.12), calls=%async_computation | async-start | bytes 1048576 | tf_op jit(solution)/shard_map/all_to_all | solution.py:104
  17.1 3.2 %copy-start.2 = (bf16[2048,2048]{1,0:T(8,128)(2,1)}, bf16[2048,2048]{1,0:T(8,128)(2,1)S(1)}, u32[]{:S(2)}) copy-start(bf16[2048,2048]{1,0:T(8,128)(2,1)S(1)} %fusion.101) | copy-start | bytes 25165828
  20.7 7.9 %copy-start.3 = (bf16[2048,2048]{1,0:T(8,128)(2,1)}, bf16[2048,2048]{1,0:T(8,128)(2,1)S(1)}, u32[]{:S(2)}) copy-start(bf16[2048,2048]{1,0:T(8,128)(2,1)S(1)} %fusion.102) | copy-start | bytes 25165828
  30.2 6.2 %slice-start = ((s8[8388608]{0:T(1024)(128)(4,1)}), s8[4194304]{0:T(1024)(128)(4,1)S(1)}, s32[]{:S(2)}) async-start(s8[8388608]{0:T(1024)(128)(4,1)} %bitcast.103), calls=%async_computation.3 | async-start | bytes 8388608
  30.5 5.9 %slice-start.1 = ((s8[8388608]{0:T(1024)(128)(4,1)}), s8[4194304]{0:T(1024)(128)(4,1)S(1)}, s32[]{:S(2)}) async-start(s8[8388608]{0:T(1024)(128)(4,1)} %bitcast.103), calls=%async_computation.4 | async-start | bytes 8388608
  41.3 23.8 %all-to-all-start.1 = ((bf16[4,128,512]{2,1,0:T(8,128)(2,1)}), bf16[4,128,512]{2,1,0:T(8,128)(2,1)S(1)}, u32[]{:S(2)}, u32[]{:S(2)}) async-start(bf16[4,128,512]{2,1,0:T(8,128)(2,1)} %bitcast.94), calls=%async_computation.1 | async-start | bytes 1048576 | tf_op jit(solution)/shard_map/all_to_all | solution.py:104
  51.4 1.6 %copy-start = (f32[256,2048]{1,0:T(8,128)S(1)}, f32[256,2048]{1,0:T(8,128)}, u32[]{:S(2)}) copy-start(f32[256,2048]{1,0:T(8,128)} %fusion.293) | copy-start | bytes 6291460
  54.2 7.1 %slice-start.2 = ((s8[8388608]{0:T(1024)(128)(4,1)}), s8[4194304]{0:T(1024)(128)(4,1)S(1)}, s32[]{:S(2)}) async-start(s8[8388608]{0:T(1024)(128)(4,1)} %bitcast.105), calls=%async_computation.5 | async-start | bytes 8388608
  55.4 5.9 %slice-start.3 = ((s8[8388608]{0:T(1024)(128)(4,1)}), s8[4194304]{0:T(1024)(128)(4,1)S(1)}, s32[]{:S(2)}) async-start(s8[8388608]{0:T(1024)(128)(4,1)} %bitcast.105), calls=%async_computation.6 | async-start | bytes 8388608
  65.1 1.6 %copy-start.1 = (f32[256,2048]{1,0:T(8,128)S(1)}, f32[256,2048]{1,0:T(8,128)}, u32[]{:S(2)}) copy-start(f32[256,2048]{1,0:T(8,128)} %fusion.44) | copy-start | bytes 6291460
  78.8 16.3 %all-to-all-start.2 = ((bf16[32,2,16,128]{3,2,1,0:T(8,128)(2,1)}), bf16[32,2,16,128]{3,2,1,0:T(8,128)(2,1)S(1)}, u32[]{:S(2)}, u32[]{:S(2)}) async-start(bf16[32,2,16,128]{3,2,1,0:T(8,128)(2,1)} %copy.33), calls=%async_computation.2 | async-start | bytes 524288 | tf_op jit(solution)/shard_map/all_to_all | solution.py:123
